TPU v7x, 256 devices: a whole 4x4x8 slice. The times are simulated.
256 devices in a mesh: grp: 8 (over z_hi, y), row: 32 (over z_lo, x, core).
Axes of the slice: x: 4, y: 4, z: 8 (z_hi: 2, z_lo: 4; z = z_hi * 4 + z_lo), core: 2. Of those that a mesh axis runs over, the one named last changes fastest.
Arguments:
- points: bfloat16 [524288, 128], P(('grp', 'row')), as said below
- centers: bfloat16 [8192, 128], replicated, as said below
- inner_factor: bfloat16 [8192, 8192], P('row'), as said below
- outer_factor: bfloat16 [8192, 8192], P('row'), as said below
- iterate: float32 [64, 8192], P(None, 'row'), may hold values from -6 to 6
- residual: float32 [64, 8192], P(None, 'row'), as said below
- direction: float32 [64, 8192], P(None, 'row'), as said below
Outputs:
- next_iterate: float32 [64, 8192], P(None, 'row')
- next_residual: float32 [64, 8192], P(None, 'row')
- next_direction: float32 [64, 8192], P(None, 'row')
Inputs may be any that keep to these rules, and one draw needn't show every extreme that they name: `inner_factor`: upper triangular: zero below the diagonal, positive on it. `outer_factor`: upper triangular: zero below the diagonal, positive on it. `residual`: finite real values. `direction`: finite real values. `points`: finite real values. `centers`: finite real values.
All inputs are finite; a program needn't handle non-finite values.
Results may differ from a plain program's by a relative error of at most 0.0056.
Values may be sent and summed in bfloat16 or wider, within the bound.
No kernel may reach another device: no remote copies, remote signals or barrier semaphores. Data moves between devices by JAX's collectives and lax.ppermute only.
A program may use at most 64 MiB of HBM per device.

v0:
```python
import jax
import jax.numpy as jnp
from jax import lax
from jax.sharding import PartitionSpec as P

ridge_weight = 0.5


def kernel_rows(block_points, centers, center_norms):
    point_wide = block_points.astype(jnp.float32)
    point_norms = jnp.sum(point_wide * point_wide, axis=1)
    cross_term = lax.dot_general(
        block_points, centers, (((1,), (1,)), ((), ())), preferred_element_type=jnp.float32
    )
    distance = point_norms[:, None] + center_norms[None, :] - 2.0 * cross_term
    return jnp.exp(distance * (-4.0 / block_points.shape[1])).astype(jnp.bfloat16)


def local(points, centers, inner_factor, outer_factor, iterate, residual, direction):
    contract_last = (((1,), (1,)), ((), ()))
    own_rows = inner_factor.shape[0]
    targets = direction.shape[0]
    direction_half = direction.astype(jnp.bfloat16)
    columns = inner_factor
    inner_term = lax.dot_general(
        lax.all_gather(direction_half, "row", axis=1, tiled=True),
        columns,
        contract_last,
        preferred_element_type=jnp.float32,
    )
    inner_half = inner_term.astype(jnp.bfloat16)
    columns = outer_factor
    outer_rows = lax.dot_general(
        lax.all_gather(inner_half, "row", axis=1, tiled=True),
        columns,
        contract_last,
        preferred_element_type=jnp.float32,
    )
    outer_half = lax.all_gather(outer_rows.astype(jnp.bfloat16), "row", axis=1, tiled=True)
    center_wide = centers.astype(jnp.float32)
    center_norms = jnp.sum(center_wide * center_wide, axis=1)
    local_points = points.shape[0]
    block_rows = min(512, local_points)
    point_blocks = points.reshape(local_points // block_rows, block_rows, points.shape[1])

    def one_block(carried, block_points):
        kernel_block = kernel_rows(block_points, centers, center_norms)
        fitted = lax.dot_general(
            outer_half, kernel_block, contract_last, preferred_element_type=jnp.float32
        ).astype(jnp.bfloat16)
        return (carried + jnp.dot(fitted, kernel_block, preferred_element_type=jnp.float32), None)

    partial_sums, _ = lax.scan(
        one_block, jnp.zeros((targets, centers.shape[0]), jnp.float32), point_blocks
    )
    summed_all = lax.psum(partial_sums, ("grp", "row"))
    own_normal = lax.dynamic_slice_in_dim(summed_all, lax.axis_index("row") * own_rows, own_rows, 1)
    normal_half = own_normal.astype(jnp.bfloat16)
    point_count = local_points * lax.axis_size("grp") * lax.axis_size("row")
    outer_terms = jnp.dot(normal_half, outer_factor, preferred_element_type=jnp.float32)
    shaped = (
        lax.psum_scatter(outer_terms, "row", scatter_dimension=1, tiled=True) / point_count
        + ridge_weight * inner_term
    )
    shaped_half = shaped.astype(jnp.bfloat16)
    inner_terms = jnp.dot(shaped_half, inner_factor, preferred_element_type=jnp.float32)
    operator_image = lax.psum_scatter(inner_terms, "row", scatter_dimension=1, tiled=True)
    old_norm = lax.psum(jnp.sum(residual * residual, axis=1), "row")
    curvature = lax.psum(jnp.sum(direction * operator_image, axis=1), "row")
    step_size = old_norm / curvature
    next_residual = residual - step_size[:, None] * operator_image
    new_norm = lax.psum(jnp.sum(next_residual * next_residual, axis=1), "row")
    next_iterate = iterate + step_size[:, None] * direction
    next_direction = next_residual + (new_norm / old_norm)[:, None] * direction
    return (next_iterate, next_residual, next_direction)


def solution(mesh):
    placed = (
        P(("grp", "row"), None),
        P(),
        P("row", None),
        P("row", None),
        P(None, "row"),
        P(None, "row"),
        P(None, "row"),
    )
    return jax.shard_map(
        local,
        mesh=mesh,
        in_specs=placed,
        out_specs=(P(None, "row"), P(None, "row"), P(None, "row")),
        check_vma=False,
    )
```

profile of v0, /device:TPU:1, one launch (start us, length us, event | category | flops | bytes accessed | tf_op | source)
XLA Modules:
  0.0 819.4 jit_solution(775019206389307324)
XLA Ops:
  7.2 1.5 convert_element_type.29
  8.7 66.0 %all-gather.4.cloned.1.call-done = bf16[64,8192]{1,0:T(8,128)(2,1)} async-done(((bf16[64,256]{1,0:T(8,128)(2,1)}), bf16[64,8192]{1,0:T(8,128)(2,1)}) %all-gather.4.cloned.1.call-update) | async-done | bytes 1048592 | tf_op jit(solution)/shard_map/all_gather | solution.py:26
  74.8 4.5 fusion.10
  79.4 59.4 %all-gather.6.cloned.1.call-done = bf16[64,8192]{1,0:T(8,128)(2,1)} async-done(((bf16[64,256]{1,0:T(8,128)(2,1)}), bf16[64,8192]{1,0:T(8,128)(2,1)}) %all-gather.6.cloned.1.call-update) | async-done | bytes 1048592 | tf_op jit(solution)/shard_map/all_gather | solution.py:34
  138.7 4.5 convolution_convert_fusion.1
  143.3 0.2 reduce-scatter.3.cloned.1.call-start
  143.5 2.7 multiply_reduce_fusion.1
  146.3 56.4 %all-gather.8.cloned.1.call-done = bf16[64,8192]{1,0:T(8,128)(2,1)} async-done(((bf16[64,256]{1,0:T(8,128)(2,1)}), bf16[64,8192]{1,0:T(8,128)(2,1)}) %all-gather.8.cloned.1.call-update) | async-done | bytes 1048592 | tf_op jit(solution)/shard_map/all_gather | solution.py:39
  202.7 87.9 %while.11 = (s32[]{:T(128)}, f32[64,8192]{1,0:T(8,128)S(1)}, bf16[4,512,128]{2,1,0:T(8,128)(2,1)}, f32[8192]{0:T(1024)S(1)}, bf16[8192,128]{1,0:T(8,128)(2,1)}, ...) while((s32[]{:T(128)}, f32[64,8192]{1,0:T(8,128)S(1)}, bf16[4,512,128]{2,1,0:T(8,128)(2,1)}, ...), condition=%wide.region_5.6_spmd.clone, body=%wide.region_3.0_spmd.clone.sunk | while | flops 2169732608 | bytes 28610700 | solution.py:53
  202.7 1.0 multiply_reduce_fusion.6
  203.7 9.0 %exponential_convert_fusion.2 = bf16[512,8192]{1,0:T(8,128)(2,1)} fusion(bf16[8192,128]{1,0:T(8,128)(2,1)} %get-tuple-element.134, f32[8192]{0:T(1024)S(1)} %get-tuple-element.133, f32[512]{0:T(512)S(1)} %multiply_reduce_fusion.6, bf16[4,512,128]{2,1,0:T(8,128)(2,1)} %get-tuple-element.132, s32[]{:T(128)S(6)} %copy.12), kind=kOutput, calls=%fused_computation.clone.1 | convolution fusion | flops 1094713344 | bytes 10651652 | tf_op jit(solution)/shard_map/while/body/eval_jaxpr/dot_general | solution.py:12
  212.8 11.9 %convolution_add_fusion.2 = f32[64,8192]{1,0:T(8,128)S(1)} fusion(bf16[512,8192]{1,0:T(8,128)(2,1)} %exponential_convert_fusion.2, f32[64,8192]{1,0:T(8,128)S(1)} %get-tuple-element.123, pred[]{:T(512)S(6)} %compare.3, bf16[64,8192]{1,0:T(8,128)(2,1)S(1)} %copy-done), kind=kOutput, calls=%fused_computation.1.clone.1 | convolution fusion | flops 1074823168 | bytes 13631489 | tf_op jit(solution)/shard_map/while/body/eval_jaxpr/dot_general | solution.py:51
  224.7 1.1 multiply_reduce_fusion.6
  225.7 9.0 %exponential_convert_fusion.2 = bf16[512,8192]{1,0:T(8,128)(2,1)} fusion(bf16[8192,128]{1,0:T(8,128)(2,1)} %get-tuple-element.134, f32[8192]{0:T(1024)S(1)} %get-tuple-element.133, f32[512]{0:T(512)S(1)} %multiply_reduce_fusion.6, bf16[4,512,128]{2,1,0:T(8,128)(2,1)} %get-tuple-element.132, s32[]{:T(128)S(6)} %copy.12), kind=kOutput, calls=%fused_computation.clone.1 | convolution fusion | flops 1094713344 | bytes 10651652 | tf_op jit(solution)/shard_map/while/body/eval_jaxpr/dot_general | solution.py:12
  234.8 11.9 %convolution_add_fusion.2 = f32[64,8192]{1,0:T(8,128)S(1)} fusion(bf16[512,8192]{1,0:T(8,128)(2,1)} %exponential_convert_fusion.2, f32[64,8192]{1,0:T(8,128)S(1)} %get-tuple-element.123, pred[]{:T(512)S(6)} %compare.3, bf16[64,8192]{1,0:T(8,128)(2,1)S(1)} %copy-done), kind=kOutput, calls=%fused_computation.1.clone.1 | convolution fusion | flops 1074823168 | bytes 13631489 | tf_op jit(solution)/shard_map/while/body/eval_jaxpr/dot_general | solution.py:51
  246.6 1.1 multiply_reduce_fusion.6
  247.7 9.0 %exponential_convert_fusion.2 = bf16[512,8192]{1,0:T(8,128)(2,1)} fusion(bf16[8192,128]{1,0:T(8,128)(2,1)} %get-tuple-element.134, f32[8192]{0:T(1024)S(1)} %get-tuple-element.133, f32[512]{0:T(512)S(1)} %multiply_reduce_fusion.6, bf16[4,512,128]{2,1,0:T(8,128)(2,1)} %get-tuple-element.132, s32[]{:T(128)S(6)} %copy.12), kind=kOutput, calls=%fused_computation.clone.1 | convolution fusion | flops 1094713344 | bytes 10651652 | tf_op jit(solution)/shard_map/while/body/eval_jaxpr/dot_general | solution.py:12
  256.7 11.9 %convolution_add_fusion.2 = f32[64,8192]{1,0:T(8,128)S(1)} fusion(bf16[512,8192]{1,0:T(8,128)(2,1)} %exponential_convert_fusion.2, f32[64,8192]{1,0:T(8,128)S(1)} %get-tuple-element.123, pred[]{:T(512)S(6)} %compare.3, bf16[64,8192]{1,0:T(8,128)(2,1)S(1)} %copy-done), kind=kOutput, calls=%fused_computation.1.clone.1 | convolution fusion | flops 1074823168 | bytes 13631489 | tf_op jit(solution)/shard_map/while/body/eval_jaxpr/dot_general | solution.py:51
  268.6 1.1 multiply_reduce_fusion.6
  269.7 9.0 %exponential_convert_fusion.2 = bf16[512,8192]{1,0:T(8,128)(2,1)} fusion(bf16[8192,128]{1,0:T(8,128)(2,1)} %get-tuple-element.134, f32[8192]{0:T(1024)S(1)} %get-tuple-element.133, f32[512]{0:T(512)S(1)} %multiply_reduce_fusion.6, bf16[4,512,128]{2,1,0:T(8,128)(2,1)} %get-tuple-element.132, s32[]{:T(128)S(6)} %copy.12), kind=kOutput, calls=%fused_computation.clone.1 | convolution fusion | flops 1094713344 | bytes 10651652 | tf_op jit(solution)/shard_map/while/body/eval_jaxpr/dot_general | solution.py:12
  278.7 11.9 %convolution_add_fusion.2 = f32[64,8192]{1,0:T(8,128)S(1)} fusion(bf16[512,8192]{1,0:T(8,128)(2,1)} %exponential_convert_fusion.2, f32[64,8192]{1,0:T(8,128)S(1)} %get-tuple-element.123, pred[]{:T(512)S(6)} %compare.3, bf16[64,8192]{1,0:T(8,128)(2,1)S(1)} %copy-done), kind=kOutput, calls=%fused_computation.1.clone.1 | convolution fusion | flops 1074823168 | bytes 13631489 | tf_op jit(solution)/shard_map/while/body/eval_jaxpr/dot_general | solution.py:51
  290.6 85.9 %all-reduce.2 = bf16[64,8192]{1,0:T(8,128)(2,1)S(1)} all-reduce(f32[64,8192]{1,0:T(8,128)S(1)} %get-tuple-element.35), channel_id=1, replica_groups=mesh['grp'=8,'row'=32] {'grp','row'}, use_global_device_ids=true, to_apply=%region_6.7 | all-reduce | flops 524288 | bytes 3145728 | tf_op jit(solution)/shard_map/psum | solution.py:56
  376.5 4.4 fusion.3
  380.9 139.3 %reduce-scatter.3.cloned.1.call-done = f32[64,256]{1,0:T(8,128)} async-done(((f32[64,8192]{1,0:T(8,128)}), f32[64,256]{1,0:T(8,128)}) %reduce-scatter.3.cloned.1.call-update) | async-done | bytes 65552 | tf_op jit(solution)/shard_map/reduce_scatter | solution.py:62
  520.3 4.5 fusion.4
  524.8 0.1 multiply_reduce_fusion.4
  524.9 144.8 %reduce-scatter.5.cloned.1.call-done = f32[64,256]{1,0:T(8,128)} async-done(((f32[64,8192]{1,0:T(8,128)}), f32[64,256]{1,0:T(8,128)}) %reduce-scatter.5.cloned.1.call-update) | async-done | bytes 65552 | tf_op jit(solution)/shard_map/reduce_scatter | solution.py:67
  669.7 0.9 multiply_reduce_fusion.3
  670.7 72.6 %all-reduce = (f32[64]{0:T(128)S(1)}, f32[64]{0:T(128)S(1)}) all-reduce(f32[64]{0:T(128)S(1)} %multiply_reduce_fusion.4, f32[64]{0:T(128)S(1)} %multiply_reduce_fusion.3), channel_id=1, replica_groups=mesh['grp'=8,'row'=32] {'row'}, use_global_device_ids=true, to_apply=%region_1.2 | all-reduce | flops 128 | bytes 1024 | tf_op jit(solution)/shard_map/psum | solution.py:68
  743.2 1.0 multiply_reduce_fusion.2
  744.3 67.9 %psum.31 = f32[64]{0:T(128)S(1)} all-reduce(f32[64]{0:T(128)S(1)} %get-tuple-element.71), channel_id=1, replica_groups=mesh['grp'=8,'row'=32] {'row'}, use_global_device_ids=true, to_apply=%region_12.13 | all-reduce | flops 64 | bytes 512 | tf_op jit(solution)/shard_map/psum | solution.py:72
  812.1 0.7 multiply_add_fusion
  (28 shorter events, 0.3 us)
Async XLA Ops:
  7.2 67.6 %all-gather.4.cloned.1.call-start = ((), (), s32[]{:S(2)}) async-start(), calls=%async_computation.2 | async-start | bytes 1081344 | tf_op jit(solution)/shard_map/all_gather | solution.py:26
  8.7 130.0 %all-gather.6.cloned.1.call-start = ((), (), s32[]{:S(2)}) async-start(), calls=%async_computation.3 | async-start | bytes 1081344 | tf_op jit(solution)/shard_map/all_gather | solution.py:34
  79.3 123.4 %all-gather.8.cloned.1.call-start = ((), (), s32[]{:S(2)}) async-start(), calls=%async_computation.4 | async-start | bytes 1081344 | tf_op jit(solution)/shard_map/all_gather | solution.py:39
  143.3 377.0 %reduce-scatter.3.cloned.1.call-start = ((), (), s32[]{:S(2)}) async-start(), calls=%async_computation.5 | async-start | bytes 2162688 | tf_op jit(solution)/shard_map/reduce_scatter | solution.py:62
  203.7 9.1 %copy-start = (bf16[64,8192]{1,0:T(8,128)(2,1)S(1)}, bf16[64,8192]{1,0:T(8,128)(2,1)}, u32[]{:S(2)}) copy-start(bf16[64,8192]{1,0:T(8,128)(2,1)} %get-tuple-element.135) | copy-start | bytes 3145732 | tf_op jit(solution)/shard_map/while
  225.7 9.1 %copy-start = (bf16[64,8192]{1,0:T(8,128)(2,1)S(1)}, bf16[64,8192]{1,0:T(8,128)(2,1)}, u32[]{:S(2)}) copy-start(bf16[64,8192]{1,0:T(8,128)(2,1)} %get-tuple-element.135) | copy-start | bytes 3145732 | tf_op jit(solution)/shard_map/while
  247.7 9.1 %copy-start = (bf16[64,8192]{1,0:T(8,128)(2,1)S(1)}, bf16[64,8192]{1,0:T(8,128)(2,1)}, u32[]{:S(2)}) copy-start(bf16[64,8192]{1,0:T(8,128)(2,1)} %get-tuple-element.135) | copy-start | bytes 3145732 | tf_op jit(solution)/shard_map/while
  269.7 9.1 %copy-start = (bf16[64,8192]{1,0:T(8,128)(2,1)S(1)}, bf16[64,8192]{1,0:T(8,128)(2,1)}, u32[]{:S(2)}) copy-start(bf16[64,8192]{1,0:T(8,128)(2,1)} %get-tuple-element.135) | copy-start | bytes 3145732 | tf_op jit(solution)/shard_map/while
  380.9 288.8 %reduce-scatter.5.cloned.1.call-start = ((), (), s32[]{:S(2)}) async-start(), calls=%async_computation.6 | async-start | bytes 2162688 | tf_op jit(solution)/shard_map/reduce_scatter | solution.py:67
  520.3 4.5 copy-start.3
  520.3 149.4 %copy-start.1 = (f32[64,256]{1,0:T(8,128)S(1)}, f32[64,256]{1,0:T(8,128)}, u32[]{:S(2)}) copy-start(f32[64,256]{1,0:T(8,128)} %param.15) | copy-start | bytes 196612
  520.3 291.8 %copy-start.4 = (f32[64,256]{1,0:T(8,128)S(1)}, f32[64,256]{1,0:T(8,128)}, u32[]{:S(2)}) copy-start(f32[64,256]{1,0:T(8,128)} %param.13) | copy-start | bytes 196612
  744.3 68.6 %copy-start.2 = (f32[64,256]{1,0:T(8,128)}, f32[64,256]{1,0:T(8,128)S(1)}, u32[]{:S(2)}) copy-start(f32[64,256]{1,0:T(8,128)S(1)} %get-tuple-element.72) | copy-start | bytes 196612
Sparse Core Ops, SparseCore 0:
  10.3 64.4 all-gather.3
  79.4 59.2 all-gather.5
  143.4 59.2 all-gather.7
  381.0 139.2 reduce-scatter.2
  524.9 144.7 reduce-scatter.4
where the time goes:
time: 820 us; the launch traced here: 819 us
  waiting for transfers between devices  466 us (57%)
  blocking collectives  226 us (28%)
  matrix products  101 us (12%)
  between operations  13.8 us (2%)
  other arithmetic  11.2 us (1%)
    reduce_scatter x1, waiting for transfers between devices, local(): lax.psum_scatter(inner_terms, 'row', scatter_dimension=1, tiled=True)  145 us
    reduce_scatter x1, waiting for transfers between devices, local(): lax.psum_scatter(outer_terms, 'row', scatter_dimension=1, tiled=True)  139 us
    psum x1, blocking collectives, local(): summed_all = lax.psum(partial_sums, ('grp', 'row'))  85.9 us
    psum x1, blocking collectives, local(): old_norm = lax.psum(jnp.sum(residual * residual, axis=1), 'row')  72.6 us
    psum x1, blocking collectives, local(): new_norm = lax.psum(jnp.sum(next_residual * next_residual, axis=1), 'row')  67.9 us
    all_gather x1, waiting for transfers between devices, local(): lax.all_gather(direction_half, 'row', axis=1, tiled=True)  66 us
    all_gather x1, waiting for transfers between devices, local(): lax.all_gather(inner_half, 'row', axis=1, tiled=True)  59.4 us
    all_gather x1, waiting for transfers between devices, local(): lax.all_gather(outer_rows.astype(jnp.bfloat16), 'row', axis=1, tiled=True)  56.4 us
  transfers between devices with their start and end apart: 5, of which 5 were waited for; matrix products, arithmetic and copies ran while one was open for 0% of the time, Pallas kernels for 0%

commit v1 on v0

--- a/solution.py
+++ b/solution.py
@@ -36,7 +36,10 @@
         contract_last,
         preferred_element_type=jnp.float32,
     )
-    outer_half = lax.all_gather(outer_rows.astype(jnp.bfloat16), "row", axis=1, tiled=True)
+    mine = outer_rows.astype(jnp.bfloat16)
+    plain = jnp.stack([mine for _ in range(lax.axis_size("row"))], 0)
+    carry = lax.all_to_all(plain, "row", split_axis=0, concat_axis=0)
+    outer_half = jnp.concatenate(carry, 1)
     center_wide = centers.astype(jnp.float32)
     center_norms = jnp.sum(center_wide * center_wide, axis=1)
     local_points = points.shape[0]

time: 820 us -> 789 us (0.962)
  waiting for transfers between devices: 466 us -> 434 us
    all_gather x1 -> x0, waiting for transfers between devices: 56.4 us -> none  [local(): lax.all_gather(outer_rows.astype(jnp.bfloat16), 'row', axis=1, tiled=True)]
    all_to_all x0 -> x1, waiting for transfers between devices: none -> 23.8 us  [local(): carry = lax.all_to_all(plain, 'row', split_axis=0, concat_axis=0)]
where the time goes in v1:
time: 789 us; the launch traced here: 788 us
  waiting for transfers between devices  434 us (55%)
  blocking collectives  226 us (29%)
  matrix products  94.3 us (12%)
  between operations  13.8 us (2%)
  other arithmetic  11.2 us (1%)
    reduce_scatter x1, waiting for transfers between devices, local(): lax.psum_scatter(inner_terms, 'row', scatter_dimension=1, tiled=True)  145 us
    reduce_scatter x1, waiting for transfers between devices, local(): lax.psum_scatter(outer_terms, 'row', scatter_dimension=1, tiled=True)  140 us
    psum x1, blocking collectives, local(): summed_all = lax.psum(partial_sums, ('grp', 'row'))  85.5 us
    psum x1, blocking collectives, local(): old_norm = lax.psum(jnp.sum(residual * residual, axis=1), 'row')  72.6 us
    psum x1, blocking collectives, local(): new_norm = lax.psum(jnp.sum(next_residual * next_residual, axis=1), 'row')  67.8 us
    all_gather x1, waiting for transfers between devices, local(): lax.all_gather(direction_half, 'row', axis=1, tiled=True)  66 us
    all_gather x1, waiting for transfers between devices, local(): lax.all_gather(inner_half, 'row', axis=1, tiled=True)  59.4 us
    dot_general x4, matrix products, one_block(): jnp.dot(fitted, kernel_block, preferred_element_type=jnp.float32)  41.1 us
  transfers between devices with their start and end apart: 5, of which 5 were waited for; matrix products, arithmetic and copies ran while one was open for 0% of the time, Pallas kernels for 0%

profile of v1, /device:TPU:1, one launch (start us, length us, event | category | flops | bytes accessed | tf_op | source)
XLA Modules:
  0.0 788.3 jit_solution(9920850863537549509)
XLA Ops:
  7.2 1.5 convert_element_type.29
  8.7 66.0 %all-gather.3.cloned.1.call-done = bf16[64,8192]{1,0:T(8,128)(2,1)} async-done(((bf16[64,256]{1,0:T(8,128)(2,1)}), bf16[64,8192]{1,0:T(8,128)(2,1)}) %all-gather.3.cloned.1.call-update) | async-done | bytes 1048592 | tf_op jit(solution)/shard_map/all_gather | solution.py:26
  74.8 4.5 fusion.10
  79.3 59.4 %all-gather.5.cloned.1.call-done = bf16[64,8192]{1,0:T(8,128)(2,1)} async-done(((bf16[64,256]{1,0:T(8,128)(2,1)}), bf16[64,8192]{1,0:T(8,128)(2,1)}) %all-gather.5.cloned.1.call-update) | async-done | bytes 1048592 | tf_op jit(solution)/shard_map/all_gather | solution.py:34
  138.7 3.9 convolution_convert_fusion.1
  142.6 1.1 stack.2
  143.7 5.3 all-to-all-start
  149.1 2.7 multiply_reduce_fusion.1
  151.8 23.8 %all-to-all-done = bf16[32,64,256]{2,1,0:T(8,128)(2,1)S(1)} async-done(((bf16[32,64,256]{2,1,0:T(8,128)(2,1)}), bf16[32,64,256]{2,1,0:T(8,128)(2,1)S(1)}, u32[]{:S(2)}, u32[]{:S(2)}) %all-to-all-start) | async-done | bytes 1048608 | tf_op jit(solution)/shard_map/all_to_all | solution.py:41
  175.7 1.0 copy-done
  176.7 1.3 copy.11
  178.0 81.3 %while.11 = (s32[]{:T(128)}, f32[64,8192]{1,0:T(8,128)S(1)}, bf16[4,512,128]{2,1,0:T(8,128)(2,1)}, f32[8192]{0:T(1024)S(1)}, bf16[8192,128]{1,0:T(8,128)(2,1)}, ...) while((s32[]{:T(128)}, f32[64,8192]{1,0:T(8,128)S(1)}, bf16[4,512,128]{2,1,0:T(8,128)(2,1)}, ...), condition=%wide.region_5.6_spmd.clone, body=%wide.region_3.0_spmd.clone.sunk | while | flops 2169732608 | bytes 24416368 | solution.py:56
  178.0 1.1 multiply_reduce_fusion.6
  179.0 9.0 %exponential_convert_fusion.2 = bf16[512,8192]{1,0:T(8,128)(2,1)} fusion(bf16[8192,128]{1,0:T(8,128)(2,1)} %get-tuple-element.134, f32[8192]{0:T(1024)S(1)} %get-tuple-element.133, f32[512]{0:T(512)S(1)} %multiply_reduce_fusion.6, bf16[4,512,128]{2,1,0:T(8,128)(2,1)} %get-tuple-element.132, s32[]{:T(128)S(6)} %copy.14), kind=kOutput, calls=%fused_computation.clone.1 | convolution fusion | flops 1094713344 | bytes 10651652 | tf_op jit(solution)/shard_map/while/body/eval_jaxpr/dot_general | solution.py:12
  188.0 10.3 %convolution_add_fusion.2 = f32[64,8192]{1,0:T(8,128)S(1)} fusion(bf16[512,8192]{1,0:T(8,128)(2,1)} %exponential_convert_fusion.2, f32[64,8192]{1,0:T(8,128)S(1)} %get-tuple-element.123, pred[]{:T(512)S(6)} %compare.3, bf16[64,8192]{1,0:T(8,128)(2,1)S(1)} %get-tuple-element.135), kind=kOutput, calls=%fused_computation.1.clone.1 | convolution fusion | flops 1074823168 | bytes 13631489 | tf_op jit(solution)/shard_map/while/body/eval_jaxpr/dot_general | solution.py:54
  198.3 1.1 multiply_reduce_fusion.6
  199.4 9.0 %exponential_convert_fusion.2 = bf16[512,8192]{1,0:T(8,128)(2,1)} fusion(bf16[8192,128]{1,0:T(8,128)(2,1)} %get-tuple-element.134, f32[8192]{0:T(1024)S(1)} %get-tuple-element.133, f32[512]{0:T(512)S(1)} %multiply_reduce_fusion.6, bf16[4,512,128]{2,1,0:T(8,128)(2,1)} %get-tuple-element.132, s32[]{:T(128)S(6)} %copy.14), kind=kOutput, calls=%fused_computation.clone.1 | convolution fusion | flops 1094713344 | bytes 10651652 | tf_op jit(solution)/shard_map/while/body/eval_jaxpr/dot_general | solution.py:12
  208.3 10.3 %convolution_add_fusion.2 = f32[64,8192]{1,0:T(8,128)S(1)} fusion(bf16[512,8192]{1,0:T(8,128)(2,1)} %exponential_convert_fusion.2, f32[64,8192]{1,0:T(8,128)S(1)} %get-tuple-element.123, pred[]{:T(512)S(6)} %compare.3, bf16[64,8192]{1,0:T(8,128)(2,1)S(1)} %get-tuple-element.135), kind=kOutput, calls=%fused_computation.1.clone.1 | convolution fusion | flops 1074823168 | bytes 13631489 | tf_op jit(solution)/shard_map/while/body/eval_jaxpr/dot_general | solution.py:54
  218.6 1.1 multiply_reduce_fusion.6
  219.7 9.0 %exponential_convert_fusion.2 = bf16[512,8192]{1,0:T(8,128)(2,1)} fusion(bf16[8192,128]{1,0:T(8,128)(2,1)} %get-tuple-element.134, f32[8192]{0:T(1024)S(1)} %get-tuple-element.133, f32[512]{0:T(512)S(1)} %multiply_reduce_fusion.6, bf16[4,512,128]{2,1,0:T(8,128)(2,1)} %get-tuple-element.132, s32[]{:T(128)S(6)} %copy.14), kind=kOutput, calls=%fused_computation.clone.1 | convolution fusion | flops 1094713344 | bytes 10651652 | tf_op jit(solution)/shard_map/while/body/eval_jaxpr/dot_general | solution.py:12
  228.7 10.3 %convolution_add_fusion.2 = f32[64,8192]{1,0:T(8,128)S(1)} fusion(bf16[512,8192]{1,0:T(8,128)(2,1)} %exponential_convert_fusion.2, f32[64,8192]{1,0:T(8,128)S(1)} %get-tuple-element.123, pred[]{:T(512)S(6)} %compare.3, bf16[64,8192]{1,0:T(8,128)(2,1)S(1)} %get-tuple-element.135), kind=kOutput, calls=%fused_computation.1.clone.1 | convolution fusion | flops 1074823168 | bytes 13631489 | tf_op jit(solution)/shard_map/while/body/eval_jaxpr/dot_general | solution.py:54
  239.0 1.1 multiply_reduce_fusion.6
  240.0 9.0 %exponential_convert_fusion.2 = bf16[512,8192]{1,0:T(8,128)(2,1)} fusion(bf16[8192,128]{1,0:T(8,128)(2,1)} %get-tuple-element.134, f32[8192]{0:T(1024)S(1)} %get-tuple-element.133, f32[512]{0:T(512)S(1)} %multiply_reduce_fusion.6, bf16[4,512,128]{2,1,0:T(8,128)(2,1)} %get-tuple-element.132, s32[]{:T(128)S(6)} %copy.14), kind=kOutput, calls=%fused_computation.clone.1 | convolution fusion | flops 1094713344 | bytes 10651652 | tf_op jit(solution)/shard_map/while/body/eval_jaxpr/dot_general | solution.py:12
  249.0 10.3 %convolution_add_fusion.2 = f32[64,8192]{1,0:T(8,128)S(1)} fusion(bf16[512,8192]{1,0:T(8,128)(2,1)} %exponential_convert_fusion.2, f32[64,8192]{1,0:T(8,128)S(1)} %get-tuple-element.123, pred[]{:T(512)S(6)} %compare.3, bf16[64,8192]{1,0:T(8,128)(2,1)S(1)} %get-tuple-element.135), kind=kOutput, calls=%fused_computation.1.clone.1 | convolution fusion | flops 1074823168 | bytes 13631489 | tf_op jit(solution)/shard_map/while/body/eval_jaxpr/dot_general | solution.py:54
  259.3 85.5 %all-reduce.2 = bf16[64,8192]{1,0:T(8,128)(2,1)S(1)} all-reduce(f32[64,8192]{1,0:T(8,128)S(1)} %get-tuple-element.35), channel_id=1, replica_groups=mesh['grp'=8,'row'=32] {'grp','row'}, use_global_device_ids=true, to_apply=%region_6.7 | all-reduce | flops 524288 | bytes 3145728 | tf_op jit(solution)/shard_map/psum | solution.py:59
  344.7 4.4 fusion.3
  349.2 140.0 %reduce-scatter.3.cloned.1.call-done = f32[64,256]{1,0:T(8,128)} async-done(((f32[64,8192]{1,0:T(8,128)}), f32[64,256]{1,0:T(8,128)}) %reduce-scatter.3.cloned.1.call-update) | async-done | bytes 65552 | tf_op jit(solution)/shard_map/reduce_scatter | solution.py:65
  489.3 4.5 fusion.4
  493.9 144.8 %reduce-scatter.5.cloned.1.call-done = f32[64,256]{1,0:T(8,128)} async-done(((f32[64,8192]{1,0:T(8,128)}), f32[64,256]{1,0:T(8,128)}) %reduce-scatter.5.cloned.1.call-update) | async-done | bytes 65552 | tf_op jit(solution)/shard_map/reduce_scatter | solution.py:70
  639.6 72.6 %all-reduce = (f32[64]{0:T(128)S(1)}, f32[64]{0:T(128)S(1)}) all-reduce(f32[64]{0:T(128)S(1)} %multiply_reduce_fusion.4, f32[64]{0:T(128)S(1)} %multiply_reduce_fusion.3), channel_id=1, replica_groups=mesh['grp'=8,'row'=32] {'row'}, use_global_device_ids=true, to_apply=%region_1.2 | all-reduce | flops 128 | bytes 1024 | tf_op jit(solution)/shard_map/psum | solution.py:71
  712.2 1.0 multiply_reduce_fusion.2
  713.2 67.8 %psum.31 = f32[64]{0:T(128)S(1)} all-reduce(f32[64]{0:T(128)S(1)} %get-tuple-element.71), channel_id=1, replica_groups=mesh['grp'=8,'row'=32] {'row'}, use_global_device_ids=true, to_apply=%region_12.13 | all-reduce | flops 64 | bytes 512 | tf_op jit(solution)/shard_map/psum | solution.py:75
  (23 shorter events, 2.1 us)
Async XLA Ops:
  7.2 67.6 %all-gather.3.cloned.1.call-start = ((), (), s32[]{:S(2)}) async-start(), calls=%async_computation.3 | async-start | bytes 1081344 | tf_op jit(solution)/shard_map/all_gather | solution.py:26
  8.7 130.0 %all-gather.5.cloned.1.call-start = ((), (), s32[]{:S(2)}) async-start(), calls=%async_computation.4 | async-start | bytes 1081344 | tf_op jit(solution)/shard_map/all_gather | solution.py:34
  143.7 31.9 %all-to-all-start = ((bf16[32,64,256]{2,1,0:T(8,128)(2,1)}), bf16[32,64,256]{2,1,0:T(8,128)(2,1)S(1)}, u32[]{:S(2)}, u32[]{:S(2)}) async-start(bf16[32,64,256]{2,1,0:T(8,128)(2,1)} %stack.2), calls=%async_computation | async-start | bytes 2097152 | tf_op jit(solution)/shard_map/all_to_all | solution.py:41
  149.0 340.2 %reduce-scatter.3.cloned.1.call-start = ((), (), s32[]{:S(2)}) async-start(), calls=%async_computation.5 | async-start | bytes 2162688 | tf_op jit(solution)/shard_map/reduce_scatter | solution.py:65
  175.7 1.0 copy-start
  349.2 289.5 %reduce-scatter.5.cloned.1.call-start = ((), (), s32[]{:S(2)}) async-start(), calls=%async_computation.6 | async-start | bytes 2162688 | tf_op jit(solution)/shard_map/reduce_scatter | solution.py:70
  489.2 4.5 copy-start.3
  489.2 149.4 %copy-start.1 = (f32[64,256]{1,0:T(8,128)S(1)}, f32[64,256]{1,0:T(8,128)}, u32[]{:S(2)}) copy-start(f32[64,256]{1,0:T(8,128)} %param.15) | copy-start | bytes 196612
  489.3 291.8 %copy-start.4 = (f32[64,256]{1,0:T(8,128)S(1)}, f32[64,256]{1,0:T(8,128)}, u32[]{:S(2)}) copy-start(f32[64,256]{1,0:T(8,128)} %param.13) | copy-start | bytes 196612
  713.2 68.6 %copy-start.2 = (f32[64,256]{1,0:T(8,128)}, f32[64,256]{1,0:T(8,128)S(1)}, u32[]{:S(2)}) copy-start(f32[64,256]{1,0:T(8,128)S(1)} %get-tuple-element.72) | copy-start | bytes 196612
Sparse Core Ops, SparseCore 0:
  10.3 64.4 all-gather.2
  79.4 59.2 all-gather.4
  349.3 139.9 reduce-scatter.2
  493.9 144.7 reduce-scatter.4
